TPU v7x, 32 devices: a whole 2x2x4 slice. The times are simulated.
32 devices in a mesh: row: 16 (over z, x, core), col: 2 (over y).
Axes of the slice: x: 2, y: 2, z: 4, core: 2. Of those that a mesh axis runs over, the one named last changes fastest.
Arguments:
- qkv: bfloat16 [256, 16, 3, 3072], P('row', 'col'), may hold values from -6 to 6
- cotangent: bfloat16 [256, 16, 3072], P('row', 'col'), may hold values from -6 to 6
- norm_gains: float32 [2, 128], replicated, may hold values from 0.1 to 1.9
- rel_table: float32 [24, 15, 15], replicated, may hold values from -6 to 250
- shifts: int32 [2], replicated, may hold values from 1 to 7
- mask_ids: int32 [256, 16], replicated, may hold values from 0 to 2
Outputs:
- attention: bfloat16 [256, 16, 3072], P('row', 'col')
- d_qkv: bfloat16 [256, 16, 3, 3072], P('row', 'col')
- d_gains: float32 [2, 128], replicated
- d_table: float32 [24, 15, 15], replicated
All inputs are finite; a program needn't handle non-finite values.
Results may differ from a plain program's by a relative error of at most 0.0073.
Values may be sent and summed in bfloat16 or wider, within the bound.
A program may use at most 192 MiB of HBM per device.

v0:
```python
import math
import jax
import jax.numpy as jnp
from jax import lax
from jax.sharding import PartitionSpec as P

EPSILON = 1e-06
NEG_FILL = -1e30


def shifted(value, axis, steps):
    count = lax.axis_size(axis)
    pairs = [(source, (source + steps) % count) for source in range(count)]
    return lax.ppermute(value, axis, pairs)


def head_norm(inputs, gain_vec):
    values = inputs.astype(jnp.float32)
    average = jnp.mean(values, axis=-1, keepdims=True)
    centred = values - average
    variance = jnp.mean(centred * centred, axis=-1, keepdims=True)
    inv_sigma = lax.rsqrt(variance + EPSILON)
    x_hat = centred * inv_sigma
    return (x_hat, inv_sigma, (x_hat * gain_vec).astype(jnp.bfloat16))


def norm_back(x_hat, inv_sigma, d_normed, gain_vec):
    d_hat = d_normed * gain_vec
    first_mean = jnp.mean(d_hat, axis=-1, keepdims=True)
    second_mean = jnp.mean(d_hat * x_hat, axis=-1, keepdims=True)
    d_input = inv_sigma * (d_hat - first_mean - x_hat * second_mean)
    d_gain = jnp.sum(d_normed * x_hat, axis=tuple(range(d_normed.ndim - 1)))
    return (d_input, d_gain)


def offset_table(window_size):
    span_count = 2 * window_size - 1
    places = jnp.arange(window_size * window_size, dtype=jnp.int32)
    row_pos = places // window_size
    col_pos = places % window_size
    code_grid = (row_pos[:, None] - row_pos[None, :] + window_size - 1) * span_count + (
        col_pos[:, None] - col_pos[None, :] + window_size - 1
    )
    codes = jnp.arange(span_count * span_count, dtype=jnp.int32)
    return (code_grid[:, :, None] == codes[None, None, :]).astype(jnp.float32)


def to_windows(field, window_size):
    row_count, col_count = (field.shape[0], field.shape[1])
    trailing = field.shape[2:]
    blocks = field.reshape(
        (row_count // window_size, window_size, col_count // window_size, window_size) + trailing
    )
    blocks = jnp.moveaxis(blocks, 2, 1)
    return blocks.reshape(
        (row_count // window_size * (col_count // window_size), window_size * window_size)
        + trailing
    )


def from_windows(blocks, window_size, row_count, col_count):
    trailing = blocks.shape[2:]
    field = blocks.reshape(
        (row_count // window_size, col_count // window_size, window_size, window_size) + trailing
    )
    field = jnp.moveaxis(field, 1, 2)
    return field.reshape((row_count, col_count) + trailing)


def window_core(q_norm, k_norm, values, grads, pos_bias, allowed, score_scale):
    scores = (
        jnp.einsum("wqhd,wkhd->whqk", q_norm, k_norm, preferred_element_type=jnp.float32)
        * score_scale
        + pos_bias[None]
    )
    scores = jnp.where(allowed[:, None], scores, NEG_FILL)
    row_max = jnp.max(scores, axis=-1, keepdims=True)
    weights = jnp.exp(scores - row_max)
    probs = weights / jnp.sum(weights, axis=-1, keepdims=True)
    probs_b = probs.astype(jnp.bfloat16)
    output = jnp.einsum("whqk,wkhd->wqhd", probs_b, values, preferred_element_type=jnp.float32)
    d_probs = jnp.einsum("wqhd,wkhd->whqk", grads, values, preferred_element_type=jnp.float32)
    row_dot = jnp.sum(probs * d_probs, axis=-1, keepdims=True)
    d_scores = probs * (d_probs - row_dot)
    d_scores_b = d_scores.astype(jnp.bfloat16)
    d_qnorm = (
        jnp.einsum("whqk,wkhd->wqhd", d_scores_b, k_norm, preferred_element_type=jnp.float32)
        * score_scale
    )
    d_knorm = (
        jnp.einsum("whqk,wqhd->wkhd", d_scores_b, q_norm, preferred_element_type=jnp.float32)
        * score_scale
    )
    d_value = jnp.einsum("whqk,wqhd->wkhd", probs_b, grads, preferred_element_type=jnp.float32)
    return (output, d_qnorm, d_knorm, d_value, jnp.sum(d_scores, axis=0))


def label_pairs(labels, window_size):
    label_win = to_windows(labels, window_size)
    return label_win[:, :, None] == label_win[:, None, :]


def local(qkv, cotangent, norm_gains, rel_table, shifts, mask_ids):
    tile_rows, tile_cols = (qkv.shape[0], qkv.shape[1])
    feature_width = qkv.shape[3]
    head_count = rel_table.shape[0]
    head_dim = feature_width // head_count
    span_count = rel_table.shape[1]
    window_size = (span_count + 1) // 2
    score_scale = 1.0 / math.sqrt(head_dim)
    shift_row = shifts[0]
    shift_col = shifts[1]
    grid_row = lax.axis_index("row") * tile_rows
    grid_col = lax.axis_index("col") * tile_cols
    one_hot = offset_table(window_size)
    pos_bias = jnp.einsum(
        "hc,qkc->hqk",
        rel_table.reshape(head_count, span_count * span_count),
        one_hot,
        precision=lax.Precision.HIGHEST,
    )
    gain_q = norm_gains[0]
    gain_k = norm_gains[1]
    stacked = jnp.concatenate([qkv, cotangent[:, :, None]], axis=2)
    received = shifted(stacked[:window_size], "row", -1)
    rolled = lax.dynamic_slice_in_dim(
        jnp.concatenate([stacked, received], axis=0), shift_row, tile_rows, 0
    )
    received = shifted(rolled, "col", -1)
    rolled = lax.dynamic_slice_in_dim(
        jnp.concatenate([rolled, received], axis=1), shift_col, tile_cols, 1
    )
    fields = rolled.reshape(tile_rows, tile_cols, 4, head_count, head_dim)
    q_hat, q_inv, q_norm = head_norm(fields[:, :, 0], gain_q)
    k_hat, k_inv, k_norm = head_norm(fields[:, :, 1], gain_k)
    labels = jnp.roll(mask_ids, (-(grid_row + shift_row), -(grid_col + shift_col)), (0, 1))[
        :tile_rows, :tile_cols
    ]
    output, d_qnorm, d_knorm, d_value, d_bias = window_core(
        to_windows(q_norm, window_size),
        to_windows(k_norm, window_size),
        to_windows(fields[:, :, 2], window_size),
        to_windows(fields[:, :, 3], window_size),
        pos_bias,
        label_pairs(labels, window_size),
        score_scale,
    )
    output = from_windows(output, window_size, tile_rows, tile_cols)
    d_qnorm = from_windows(d_qnorm, window_size, tile_rows, tile_cols)
    d_knorm = from_windows(d_knorm, window_size, tile_rows, tile_cols)
    d_value = from_windows(d_value, window_size, tile_rows, tile_cols)
    d_query, dgain_q = norm_back(q_hat, q_inv, d_qnorm, gain_q)
    d_key, dgain_k = norm_back(k_hat, k_inv, d_knorm, gain_k)
    results = (
        jnp.stack([output, d_query, d_key, d_value], axis=2)
        .reshape(tile_rows, tile_cols, 4, feature_width)
        .astype(jnp.bfloat16)
    )
    received = shifted(results[tile_rows - window_size :], "row", 1)
    results = lax.dynamic_slice_in_dim(
        jnp.concatenate([received, results], axis=0), window_size - shift_row, tile_rows, 0
    )
    received = shifted(results, "col", 1)
    results = lax.dynamic_slice_in_dim(
        jnp.concatenate([received, results], axis=1), window_size - shift_col, tile_cols, 1
    )
    attention = results[:, :, 0]
    d_qkv = results[:, :, 1:]
    table_local = jnp.einsum("hqk,qkc->hc", d_bias, one_hot, precision=lax.Precision.HIGHEST)
    totals = lax.psum((jnp.stack([dgain_q, dgain_k]), table_local), ("row", "col"))
    return (attention, d_qkv, totals[0], totals[1].reshape(head_count, span_count, span_count))


def solution(mesh):
    placed = (P("row", "col", None, None), P("row", "col", None), P(), P(), P(), P())
    return jax.shard_map(
        local,
        mesh=mesh,
        in_specs=placed,
        out_specs=(P("row", "col", None), P("row", "col", None, None), P(), P()),
        check_vma=False,
    )
```

profile of v0, /device:TPU:0, one launch (start us, length us, event | category | flops | bytes accessed | tf_op | source)
XLA Modules:
  0.0 298.4 jit_solution(15147776239652918049)
XLA Ops:
  0.6 1.5 pad_maximum_fusion
  2.2 5.5 %collective-permute-start = (bf16[8,8,4,3072]{3,1,2,0:T(8,128)(2,1)S(1)}, bf16[8,8,4,3072]{3,1,2,0:T(8,128)(2,1)}, u32[]{:S(2)}, u32[]{:S(2)}) collective-permute-start(bf16[8,8,4,3072]{3,1,2,0:T(8,128)(2,1)S(1)} %pad_maximum_fusion), channel_id=1, source_target_pairs={{0,30},{2,0},{4,2},{6,4},{8,6},{10,8},{12,10},{14,12},{16,14},{18,... | collective-permute-start | bytes 4718600 | tf_op jit(solution)/shard_map/ppermute | solution.py:14
  7.7 0.6 fusion.39
  10.2 15.4 %collective-permute-done = bf16[8,8,4,3072]{3,1,2,0:T(8,128)(2,1)} collective-permute-done((bf16[8,8,4,3072]{3,1,2,0:T(8,128)(2,1)S(1)}, bf16[8,8,4,3072]{3,1,2,0:T(8,128)(2,1)}, u32[]{:S(2)}, u32[]{:S(2)}) %collective-permute-start) | collective-permute-done | bytes 1572896 | tf_op jit(solution)/shard_map/ppermute | solution.py:14
  25.6 2.9 fusion.5
  28.5 1.6 collective-permute-start.1
  32.5 0.1 fusion.34
  32.6 0.1 copy.44
  32.7 0.1 eq.45
  32.8 0.1 add_add_fusion
  32.9 0.6 copy-done.11
  33.5 0.9 iota_compare_fusion
  34.4 4.5 %fusion.20 = f32[24,64,64]{2,0,1:T(8,128)} fusion(pred[64,64,225]{2,0,1:T(32,128)(4,1)S(1)} %iota_compare_fusion, f32[24,225]{0,1:T(8,128)S(1)} %reshape.290), kind=kOutput, calls=%fused_computation.52 | convolution fusion | flops 265420800 | bytes 1336416 | tf_op jit(solution)/shard_map/hc,qkc->hqk/dot_general | solution.py:116
  38.9 2.3 copy.53
  41.8 0.6 broadcast_multiply_fusion.6
  42.4 0.7 broadcast_compare_fusion
  43.1 53.5 %collective-permute-done.1 = bf16[16,8,4,3072]{3,1,2,0:T(8,128)(2,1)} collective-permute-done((bf16[16,8,4,3072]{3,1,2,0:T(8,128)(2,1)S(1)}, bf16[16,8,4,3072]{3,1,2,0:T(8,128)(2,1)}, u32[]{:S(2)}, u32[]{:S(2)}) %collective-permute-start.1) | collective-permute-done | bytes 3145760 | tf_op jit(solution)/shard_map/ppermute | solution.py:14
  96.6 4.0 %fusion.7 = bf16[16,8,4,3072]{3,1,2,0:T(8,128)(2,1)S(1)} fusion(s32[]{:T(128)S(6)} %select_n.71, bf16[16,8,4,3072]{3,1,2,0:T(8,128)(2,1)S(1)} %fusion.5, bf16[16,8,4,3072]{3,1,2,0:T(8,128)(2,1)} %collective-permute-done.1), kind=kLoop, calls=%fused_computation.17 | loop fusion | flops 6291456 | bytes 9437188 | tf_op jit(solution)/shard_map/concatenate | solution.py:131
  100.6 0.9 copy.76
  101.5 0.9 convert_reduce_fusion
  102.4 2.4 fusion.38
  104.8 1.9 fusion.12
  107.0 4.2 %add_select_fusion = f32[2,24,64,64]{2,3,1,0:T(8,128)S(1)} fusion(f32[24,64,64]{1,2,0:T(8,128)} %copy.53, pred[2,64,64]{1,2,0:T(8,128)(4,1)} %broadcast_compare_fusion, f32[2,64,24,128]{3,2,1,0:T(8,128)} %bitcast.113, f32[128]{0:T(128)S(1)} %get-tuple-element.35, f32[2,64,24]{1,2,0:T(8,128)S(1)} %copy.47, f32[2,64,24]{1,2,0:T(8,128)S(1)} %copy.45, ...), kind=kOutput, calls=%fused_computation.44 | convolution fusion | flops 54067200 | bytes 4383744 | tf_op jit(solution)/shard_map/wqhd,wkhd->whqk/dot_general | solution.py:72
  111.2 1.6 fusion.40
  112.9 3.6 %fusion.19 = bf16[2,64,24,128]{3,1,2,0:T(8,128)(2,1)} fusion(bf16[2,64,24,128]{3,2,1,0:T(8,128)(2,1)} %bitcast.120, f32[2,24,64]{2,1,0:T(8,128)S(1)} %get-tuple-element.38, f32[2,24,64,64]{2,3,1,0:T(8,128)} %copy-done.2), kind=kOutput, calls=%fused_computation.51 | convolution fusion | flops 51317824 | bytes 2371584 | tf_op jit(solution)/shard_map/whqk,wqhd->wkhd/dot_general | solution.py:94
  116.5 3.6 %fusion.18 = bf16[2,64,24,128]{3,1,2,0:T(8,128)(2,1)} fusion(bf16[2,64,24,128]{3,2,1,0:T(8,128)(2,1)} %bitcast.122, f32[2,24,64]{2,1,0:T(8,128)S(1)} %get-tuple-element.38, f32[2,24,64,64]{2,3,1,0:T(8,128)} %copy-done.2), kind=kOutput, calls=%fused_computation.50 | convolution fusion | flops 51317824 | bytes 2371584 | tf_op jit(solution)/shard_map/whqk,wkhd->wqhd/dot_general | solution.py:81
  120.1 2.5 copy.56
  122.6 2.2 stack.22
  124.8 2.5 copy.69
  127.3 2.2 stack.25
  129.5 2.6 multiply_reduce_fusion.2
  132.1 1.4 fusion.29
  133.5 0.7 copy-done.4
  134.2 4.8 %multiply_reduce_fusion = (f32[128]{0:T(128)}, f32[2,64,24]{1,2,0:T(8,128)S(1)}, f32[2,64,24]{1,2,0:T(8,128)S(1)}, f32[2,24,128,64]{2,3,1,0:T(8,128)}) fusion(f32[2,64,24,128]{3,2,1,0:T(8,128)S(1)} %bitcast.111, f32[2,64,24]{1,2,0:T(8,128)S(1)} %copy.50, f32[2,64,24]{1,2,0:T(8,128)S(1)} %copy.48, f32[128]{0:T(128)S(1)} %copy-done.20, ...), kind=kOutput, calls=%fused_computation.36 | convolution fusion | flops 55437184 | bytes 5187072 | tf_op jit(solution)/shard_map/whqk,wqhd->wkhd/dot_general | solution.py:91
  139.0 5.3 %multiply_reduce_fusion.1 = (f32[128]{0:T(128)}, f32[2,64,24]{1,2,0:T(8,128)S(1)}, f32[2,64,24]{1,2,0:T(8,128)S(1)}, f32[2,24,128,64]{2,3,1,0:T(8,128)}) fusion(f32[2,64,24,128]{3,2,1,0:T(8,128)S(1)} %bitcast.115, f32[2,64,24]{1,2,0:T(8,128)S(1)} %copy.47, f32[2,64,24]{1,2,0:T(8,128)S(1)} %copy.45, f32[128]{0:T(128)S(1)} %copy-done.19, ...), kind=kOutput, calls=%fused_computation.37 | convolution fusion | flops 55437184 | bytes 5187072 | tf_op jit(solution)/shard_map/whqk,wkhd->wqhd/dot_general | solution.py:87
  144.3 0.6 broadcast_multiply_fusion.2
  144.9 0.6 broadcast_multiply_fusion.3
  145.5 0.6 broadcast_multiply_fusion.4
  146.2 0.1 copy.62
  146.2 0.8 copy.63
  147.1 1.4 copy.66
  148.5 1.4 copy.67
  149.9 1.6 multiply_bitcast_fusion
  151.5 0.9 copy.64
  152.4 0.5 copy-done.8
  152.9 0.2 multiply_bitcast_fusion.1
  153.2 0.9 copy.60
  154.1 5.1 %multiply_convert_fusion = (bf16[16,8,1,24,128]{4,3,1,2,0:T(8,128)(2,1)}, bf16[16,8,1,24,128]{4,3,1,2,0:T(8,128)(2,1)}) fusion(f32[16,8,1,24,128]{4,3,1,2,0:T(8,128)S(1)} %bitcast.108, f32[16,8,24]{2,1,0:T(8,128)S(1)} %bitcast.129, f32[16,8,24]{2,1,0:T(8,128)S(1)} %get-tuple-element.46, f32[16,8,24]{2,1,0:T(8,128)S(1)} %bitcast.128, ...), kind=kLoop, calls=%fused_computation.38 | loop fusion | flops 7077888 | bytes 6390784 | tf_op jit(solution)/shard_map/convert.8
  159.2 1.5 stack.24
  160.8 0.3 stack.23
  161.3 1.0 copy-done.5
  162.4 0.1 slice.56
  162.5 1.5 copy-done
  165.4 21.3 %collective-permute-done.2 = bf16[8,8,4,3072]{3,1,0,2:T(8,128)(2,1)} collective-permute-done((bf16[8,8,4,3072]{3,1,0,2:T(8,128)(2,1)S(1)}, bf16[8,8,4,3072]{3,1,0,2:T(8,128)(2,1)}, u32[]{:S(2)}, u32[]{:S(2)}) %collective-permute-start.2) | collective-permute-done | bytes 1572896 | tf_op jit(solution)/shard_map/ppermute | solution.py:14
  186.7 2.6 fusion.3
  189.3 1.6 collective-permute-start.3
  192.1 2.8 convolution_bitcast_fusion
  194.9 0.1 reshape.285
  195.0 95.8 %all-reduce = (f32[2,128]{1,0:T(2,128)}, f32[24,15,15]{2,1,0:T(8,128)S(1)}) all-reduce(f32[2,128]{1,0:T(2,128)S(1)} %pad_maximum_fusion.1, f32[24,15,15]{2,1,0:T(8,128)S(1)} %reshape.285), channel_id=1, replica_groups=mesh['row'=16,'col'=2] {'row','col'}, use_global_device_ids=true, to_apply=%region_13.14 | all-reduce | flops 5656 | bytes 45248 | tf_op jit(solution)/shard_map/psum | solution.py:170
  290.9 0.8 copy.72
  291.7 4.0 %fusion.6 = bf16[16,8,4,3072]{3,1,0,2:T(8,128)(2,1)S(1)} fusion(s32[]{:T(128)S(6)} %select_n.80, bf16[16,8,4,3072]{3,1,0,2:T(8,128)(2,1)} %collective-permute-done.3, bf16[16,8,4,3072]{3,1,0,2:T(8,128)(2,1)S(1)} %fusion.3), kind=kLoop, calls=%fused_computation.16 | loop fusion | flops 6291456 | bytes 9437188 | tf_op jit(solution)/shard_map/concatenate | solution.py:165
  295.8 0.9 slice_bitcast_fusion
  296.7 0.2 slice.58
  296.8 1.6 copy.71
  (56 shorter events, 0.7 us)
Async XLA Ops:
  0.6 7.1 %copy-start.16 = (s32[2]{0:T(128)S(1)}, s32[2]{0:T(128)}, u32[]{:S(2)}) copy-start(s32[2]{0:T(128)} %param.10) | copy-start | bytes 28
  2.2 23.4 %collective-permute-start = (bf16[8,8,4,3072]{3,1,2,0:T(8,128)(2,1)S(1)}, bf16[8,8,4,3072]{3,1,2,0:T(8,128)(2,1)}, u32[]{:S(2)}, u32[]{:S(2)}) collective-permute-start(bf16[8,8,4,3072]{3,1,2,0:T(8,128)(2,1)S(1)} %pad_maximum_fusion), channel_id=1, source_target_pairs={{0,30},{2,0},{4,2},{6,4},{8,6},{10,8},{12,10},{14,12},{16,14},{18,... | collective-permute-start | bytes 4718600 | tf_op jit(solution)/shard_map/ppermute | solution.py:14
  10.2 22.3 %copy-start.14 = (s32[256,16]{0,1:T(8,128)S(1)}, s32[256,16]{0,1:T(8,128)}, u32[]{:S(2)}) copy-start(s32[256,16]{0,1:T(8,128)} %param.11) | copy-start | bytes 49156
  10.2 22.5 %copy-start.13 = (f32[24,15,15]{0,2,1:T(8,128)S(1)}, f32[24,15,15]{0,2,1:T(8,128)}, u32[]{:S(2)}) copy-start(f32[24,15,15]{0,2,1:T(8,128)} %param.9) | copy-start | bytes 64804
  28.5 68.1 %collective-permute-start.1 = (bf16[16,8,4,3072]{3,1,2,0:T(8,128)(2,1)S(1)}, bf16[16,8,4,3072]{3,1,2,0:T(8,128)(2,1)}, u32[]{:S(2)}, u32[]{:S(2)}) collective-permute-start(bf16[16,8,4,3072]{3,1,2,0:T(8,128)(2,1)S(1)} %fusion.5), channel_id=1, source_target_pairs={{0,1},{1,0},{2,3},{3,2},{4,5},{5,4},{6,7},{7,6},{8,9},{9,8},{10,11... | collective-permute-start | bytes 9437192 | tf_op jit(solution)/shard_map/ppermute | solution.py:14
  32.9 0.6 copy-start.11
  38.9 2.9 copy-start.15
  111.2 1.7 copy-start.2
  129.5 2.6 copy-start.1
  132.1 1.4 copy-start.3
  132.1 2.2 copy-start.4
  132.1 2.1 copy-start.20
  134.2 4.8 %copy-start.19 = (f32[128]{0:T(128)S(1)}, f32[128]{0:T(128)}, u32[]{:S(2)}) copy-start(f32[128]{0:T(128)} %get-tuple-element.33) | copy-start | bytes 1540
  151.5 1.4 copy-start.8
  153.2 0.9 copy-start.9
  153.2 0.9 copy-start.10
  159.2 1.6 copy-start.7
  159.2 1.9 copy-start.6
  161.2 1.1 copy-start.5
  162.4 1.7 copy-start
  164.1 22.6 %collective-permute-start.2 = (bf16[8,8,4,3072]{3,1,0,2:T(8,128)(2,1)S(1)}, bf16[8,8,4,3072]{3,1,0,2:T(8,128)(2,1)}, u32[]{:S(2)}, u32[]{:S(2)}) collective-permute-start(bf16[8,8,4,3072]{3,1,0,2:T(8,128)(2,1)S(1)} %slice.56), channel_id=1, source_target_pairs={{0,2},{2,4},{4,6},{6,8},{8,10},{10,12},{12,14},{14,16},{16,18},{18... | collective-permute-start | bytes 4718600 | tf_op jit(solution)/shard_map/ppermute | solution.py:14
  165.4 26.7 %copy-start.12 = (s32[64,64]{0,1:T(8,128)S(1)}, s32[64,64]{0,1:T(8,128)}, u32[]{:S(2)}) copy-start(s32[64,64]{0,1:T(8,128)} %copy-done.11) | copy-start | bytes 49156
  189.3 5.7 %copy-start.17 = (f32[128]{0:T(128)S(1)}, f32[128]{0:T(128)}, u32[]{:S(2)}) copy-start(f32[128]{0:T(128)} %get-tuple-element.14) | copy-start | bytes 1540
  189.3 5.7 %copy-start.18 = (f32[128]{0:T(128)S(1)}, f32[128]{0:T(128)}, u32[]{:S(2)}) copy-start(f32[128]{0:T(128)} %get-tuple-element.12) | copy-start | bytes 1540
  189.3 102.4 %collective-permute-start.3 = (bf16[16,8,4,3072]{3,1,0,2:T(8,128)(2,1)S(1)}, bf16[16,8,4,3072]{3,1,0,2:T(8,128)(2,1)}, u32[]{:S(2)}, u32[]{:S(2)}) collective-permute-start(bf16[16,8,4,3072]{3,1,0,2:T(8,128)(2,1)S(1)} %fusion.3), channel_id=1, source_target_pairs={{0,1},{1,0},{2,3},{3,2},{4,5},{5,4},{6,7},{7,6},{8,9},{9,8},{10,11... | collective-permute-start | bytes 9437192 | tf_op jit(solution)/shard_map/ppermute | solution.py:14
where the time goes:
time: 299 us; the launch traced here: 298 us
  blocking collectives  95.8 us (32%)
  waiting for transfers between devices  90.2 us (30%)
  other arithmetic  34.4 us (12%)
  matrix products  31.4 us (11%)
  local copies, waits for them, and re-layouts  29.4 us (10%)
  starting transfers between devices  8.67 us (3%)
  between operations  8.46 us (3%)
    psum x1, blocking collectives, local(): lax.psum((jnp.stack([dgain_q, dgain_k]), table_local), ('row', 'col'))  95.8 us
    ppermute x4, waiting for transfers between devices, shifted(): return lax.ppermute(value, axis, pairs)  90.2 us
    ppermute x4, starting transfers between devices, shifted(): return lax.ppermute(value, axis, pairs)  8.67 us
    unnamed x48, local copies, waits for them, and re-layouts  7.83 us
    another operation x5, local copies, waits for them, and re-layouts, local(): jnp.stack([output, d_query, d_key, d_value], axis=2)  6.26 us
  transfers between devices with their start and end apart: 4, of which 3 were waited for; matrix products, arithmetic and copies ran while one was open for 5% of the time, Pallas kernels for 0%

commit v1 on v0

--- a/solution.py
+++ b/solution.py
@@ -167,7 +167,7 @@
     attention = results[:, :, 0]
     d_qkv = results[:, :, 1:]
     table_local = jnp.einsum("hqk,qkc->hc", d_bias, one_hot, precision=lax.Precision.HIGHEST)
-    totals = lax.psum((jnp.stack([dgain_q, dgain_k]), table_local), ("row", "col"))
+    totals = lax.psum(lax.psum((jnp.stack([dgain_q, dgain_k]), table_local), "row"), "col")
     return (attention, d_qkv, totals[0], totals[1].reshape(head_count, span_count, span_count))
 
 

time: 299 us -> 271 us (0.906)
  blocking collectives: 95.8 us -> 67.6 us
    psum x1 -> x2, blocking collectives: 95.8 us -> 67.6 us  [the longest x1 57.6 us: local(): lax.psum((jnp.stack([dgain_q, dgain_k]), table_local), 'row')]
where the time goes in v1:
time: 271 us; the launch traced here: 270 us
  waiting for transfers between devices  90.2 us (33%)
  blocking collectives  67.6 us (25%)
  other arithmetic  34.4 us (13%)
  matrix products  31.4 us (12%)
  local copies, waits for them, and re-layouts  29.4 us (11%)
  starting transfers between devices  8.67 us (3%)
  between operations  8.45 us (3%)
    ppermute x4, waiting for transfers between devices, shifted(): return lax.ppermute(value, axis, pairs)  90.2 us
    psum x1, blocking collectives, local(): lax.psum((jnp.stack([dgain_q, dgain_k]), table_local), 'row')  57.6 us
    psum x1, blocking collectives, local(): lax.psum(lax.psum((jnp.stack([dgain_q, dgain_k]), table_local), 'row'), '...  9.96 us
    ppermute x4, starting transfers between devices, shifted(): return lax.ppermute(value, axis, pairs)  8.67 us
    unnamed x48, local copies, waits for them, and re-layouts  7.83 us
    another operation x5, local copies, waits for them, and re-layouts, local(): jnp.stack([output, d_query, d_key, d_value], axis=2)  6.26 us
  transfers between devices with their start and end apart: 4, of which 3 were waited for; matrix products, arithmetic and copies ran while one was open for 5% of the time, Pallas kernels for 0%

profile of v1, /device:TPU:0, one launch (start us, length us, event | category | flops | bytes accessed | tf_op | source)
XLA Modules:
  0.0 270.1 jit_solution(16778575518963920189)
XLA Ops:
  0.6 1.5 pad_maximum_fusion
  2.2 5.5 %collective-permute-start = (bf16[8,8,4,3072]{3,1,2,0:T(8,128)(2,1)S(1)}, bf16[8,8,4,3072]{3,1,2,0:T(8,128)(2,1)}, u32[]{:S(2)}, u32[]{:S(2)}) collective-permute-start(bf16[8,8,4,3072]{3,1,2,0:T(8,128)(2,1)S(1)} %pad_maximum_fusion), channel_id=1, source_target_pairs={{0,30},{2,0},{4,2},{6,4},{8,6},{10,8},{12,10},{14,12},{16,14},{18,... | collective-permute-start | bytes 4718600 | tf_op jit(solution)/shard_map/ppermute | solution.py:14
  7.7 0.6 fusion.39
  10.2 15.4 %collective-permute-done = bf16[8,8,4,3072]{3,1,2,0:T(8,128)(2,1)} collective-permute-done((bf16[8,8,4,3072]{3,1,2,0:T(8,128)(2,1)S(1)}, bf16[8,8,4,3072]{3,1,2,0:T(8,128)(2,1)}, u32[]{:S(2)}, u32[]{:S(2)}) %collective-permute-start) | collective-permute-done | bytes 1572896 | tf_op jit(solution)/shard_map/ppermute | solution.py:14
  25.6 2.9 %fusion.5 = bf16[16,8,4,3072]{3,1,2,0:T(8,128)(2,1)S(1)} fusion(s32[]{:T(128)S(6)} %select_n.70, bf16[16,8,3,3072]{3,1,2,0:T(8,128)(2,1)} %param.6, bf16[16,8,1,3072]{3,1,2,0:T(8,128)(2,1)} %bitcast.117, bf16[8,8,4,3072]{3,1,2,0:T(8,128)(2,1)} %collective-permute-done), kind=kLoop, calls=%fused_computation.15 | loop fusion | flops 3145728 | bytes 7864324 | tf_op jit(solution)/shard_map/concatenate | solution.py:127
  28.5 1.6 collective-permute-start.1
  32.5 0.1 fusion.34
  32.7 0.1 eq.45
  32.8 0.1 add_add_fusion
  32.9 0.6 copy-done.11
  33.5 0.9 iota_compare_fusion
  34.4 4.5 %fusion.20 = f32[24,64,64]{2,0,1:T(8,128)} fusion(pred[64,64,225]{2,0,1:T(32,128)(4,1)S(1)} %iota_compare_fusion, f32[24,225]{0,1:T(8,128)S(1)} %reshape.290), kind=kOutput, calls=%fused_computation.52 | convolution fusion | flops 265420800 | bytes 1336416 | tf_op jit(solution)/shard_map/hc,qkc->hqk/dot_general | solution.py:116
  38.9 2.3 copy.53
  41.8 0.6 broadcast_multiply_fusion.6
  42.4 0.7 broadcast_compare_fusion
  43.1 53.5 %collective-permute-done.1 = bf16[16,8,4,3072]{3,1,2,0:T(8,128)(2,1)} collective-permute-done((bf16[16,8,4,3072]{3,1,2,0:T(8,128)(2,1)S(1)}, bf16[16,8,4,3072]{3,1,2,0:T(8,128)(2,1)}, u32[]{:S(2)}, u32[]{:S(2)}) %collective-permute-start.1) | collective-permute-done | bytes 3145760 | tf_op jit(solution)/shard_map/ppermute | solution.py:14
  96.6 4.0 %fusion.7 = bf16[16,8,4,3072]{3,1,2,0:T(8,128)(2,1)S(1)} fusion(s32[]{:T(128)S(6)} %select_n.71, bf16[16,8,4,3072]{3,1,2,0:T(8,128)(2,1)S(1)} %fusion.5, bf16[16,8,4,3072]{3,1,2,0:T(8,128)(2,1)} %collective-permute-done.1), kind=kLoop, calls=%fused_computation.17 | loop fusion | flops 6291456 | bytes 9437188 | tf_op jit(solution)/shard_map/concatenate | solution.py:131
  100.6 0.9 copy.76
  101.5 0.9 convert_reduce_fusion
  102.4 2.4 fusion.38
  104.8 1.9 fusion.12
  107.0 4.2 %add_select_fusion = f32[2,24,64,64]{2,3,1,0:T(8,128)S(1)} fusion(f32[24,64,64]{1,2,0:T(8,128)} %copy.53, pred[2,64,64]{1,2,0:T(8,128)(4,1)} %broadcast_compare_fusion, f32[2,64,24,128]{3,2,1,0:T(8,128)} %bitcast.113, f32[128]{0:T(128)S(1)} %get-tuple-element.37, f32[2,64,24]{1,2,0:T(8,128)S(1)} %copy.47, f32[2,64,24]{1,2,0:T(8,128)S(1)} %copy.45, ...), kind=kOutput, calls=%fused_computation.44 | convolution fusion | flops 54067200 | bytes 4383744 | tf_op jit(solution)/shard_map/wqhd,wkhd->whqk/dot_general | solution.py:72
  111.2 1.6 fusion.40
  112.9 3.6 %fusion.19 = bf16[2,64,24,128]{3,1,2,0:T(8,128)(2,1)} fusion(bf16[2,64,24,128]{3,2,1,0:T(8,128)(2,1)} %bitcast.120, f32[2,24,64]{2,1,0:T(8,128)S(1)} %get-tuple-element.40, f32[2,24,64,64]{2,3,1,0:T(8,128)} %copy-done.2), kind=kOutput, calls=%fused_computation.51 | convolution fusion | flops 51317824 | bytes 2371584 | tf_op jit(solution)/shard_map/whqk,wqhd->wkhd/dot_general | solution.py:94
  116.5 3.6 %fusion.18 = bf16[2,64,24,128]{3,1,2,0:T(8,128)(2,1)} fusion(bf16[2,64,24,128]{3,2,1,0:T(8,128)(2,1)} %bitcast.122, f32[2,24,64]{2,1,0:T(8,128)S(1)} %get-tuple-element.40, f32[2,24,64,64]{2,3,1,0:T(8,128)} %copy-done.2), kind=kOutput, calls=%fused_computation.50 | convolution fusion | flops 51317824 | bytes 2371584 | tf_op jit(solution)/shard_map/whqk,wkhd->wqhd/dot_general | solution.py:81
  120.1 2.5 copy.56
  122.6 2.2 stack.22
  124.8 2.5 copy.69
  127.3 2.2 stack.25
  129.5 2.6 multiply_reduce_fusion.2
  132.1 1.4 fusion.29
  133.5 0.7 copy-done.4
  134.2 4.8 %multiply_reduce_fusion = (f32[128]{0:T(128)}, f32[2,64,24]{1,2,0:T(8,128)S(1)}, f32[2,64,24]{1,2,0:T(8,128)S(1)}, f32[2,24,128,64]{2,3,1,0:T(8,128)}) fusion(f32[2,64,24,128]{3,2,1,0:T(8,128)S(1)} %bitcast.111, f32[2,64,24]{1,2,0:T(8,128)S(1)} %copy.50, f32[2,64,24]{1,2,0:T(8,128)S(1)} %copy.48, f32[128]{0:T(128)S(1)} %copy-done.20, ...), kind=kOutput, calls=%fused_computation.36 | convolution fusion | flops 55437184 | bytes 5187072 | tf_op jit(solution)/shard_map/whqk,wqhd->wkhd/dot_general | solution.py:91
  139.0 5.3 %multiply_reduce_fusion.1 = (f32[128]{0:T(128)}, f32[2,64,24]{1,2,0:T(8,128)S(1)}, f32[2,64,24]{1,2,0:T(8,128)S(1)}, f32[2,24,128,64]{2,3,1,0:T(8,128)}) fusion(f32[2,64,24,128]{3,2,1,0:T(8,128)S(1)} %bitcast.115, f32[2,64,24]{1,2,0:T(8,128)S(1)} %copy.47, f32[2,64,24]{1,2,0:T(8,128)S(1)} %copy.45, f32[128]{0:T(128)S(1)} %copy-done.19, ...), kind=kOutput, calls=%fused_computation.37 | convolution fusion | flops 55437184 | bytes 5187072 | tf_op jit(solution)/shard_map/whqk,wkhd->wqhd/dot_general | solution.py:87
  144.3 0.6 broadcast_multiply_fusion.2
  144.9 0.6 broadcast_multiply_fusion.3
  145.5 0.6 broadcast_multiply_fusion.4
  146.2 0.1 copy.62
  146.2 0.8 copy.63
  147.1 1.4 copy.66
  148.5 1.4 copy.67
  149.9 1.6 multiply_bitcast_fusion
  151.5 0.9 copy.64
  152.4 0.5 copy-done.8
  152.9 0.2 multiply_bitcast_fusion.1
  153.2 0.9 copy.60
  154.1 5.1 %multiply_convert_fusion = (bf16[16,8,1,24,128]{4,3,1,2,0:T(8,128)(2,1)}, bf16[16,8,1,24,128]{4,3,1,2,0:T(8,128)(2,1)}) fusion(f32[16,8,1,24,128]{4,3,1,2,0:T(8,128)S(1)} %bitcast.108, f32[16,8,24]{2,1,0:T(8,128)S(1)} %bitcast.129, f32[16,8,24]{2,1,0:T(8,128)S(1)} %get-tuple-element.48, f32[16,8,24]{2,1,0:T(8,128)S(1)} %bitcast.128, ...), kind=kLoop, calls=%fused_computation.38 | loop fusion | flops 7077888 | bytes 6390784 | tf_op jit(solution)/shard_map/convert.8
  159.2 1.5 stack.24
  160.8 0.3 stack.23
  161.3 1.0 copy-done.5
  162.4 0.1 slice.56
  162.5 1.5 copy-done
  165.4 21.3 %collective-permute-done.2 = bf16[8,8,4,3072]{3,1,0,2:T(8,128)(2,1)} collective-permute-done((bf16[8,8,4,3072]{3,1,0,2:T(8,128)(2,1)S(1)}, bf16[8,8,4,3072]{3,1,0,2:T(8,128)(2,1)}, u32[]{:S(2)}, u32[]{:S(2)}) %collective-permute-start.2) | collective-permute-done | bytes 1572896 | tf_op jit(solution)/shard_map/ppermute | solution.py:14
  186.7 2.6 fusion.3
  189.3 1.6 collective-permute-start.3
  192.1 2.8 %convolution_bitcast_fusion = f32[24,225]{1,0:T(8,128)S(1)} fusion(f32[24,64,64]{1,2,0:T(8,128)} %get-tuple-element.26, s32[64,64]{0,1:T(8,128)S(1)} %copy-done.12), kind=kOutput, calls=%fused_computation.55 | convolution fusion | flops 266342400 | bytes 431200 | tf_op jit(solution)/shard_map/hqk,qkc->hc/dot_general | solution.py:169
  194.9 57.6 %all-reduce = (f32[2,128]{1,0:T(2,128)S(1)}, f32[24,225]{1,0:T(8,128)S(1)}) all-reduce(f32[2,128]{1,0:T(2,128)S(1)} %pad_maximum_fusion.1, f32[24,225]{1,0:T(8,128)S(1)} %convolution_bitcast_fusion), channel_id=1, replica_groups=mesh['row'=16,'col'=2] {'row'}, use_global_device_ids=true, to_apply=%region_13.14 | all-reduce | flops 5656 | bytes 45248 | tf_op jit(solution)/shard_map/psum | solution.py:170
  252.5 0.1 reshape.285
  252.7 10.0 %all-reduce.1 = (f32[2,128]{1,0:T(2,128)}, f32[24,15,15]{2,1,0:T(8,128)S(1)}) all-reduce(f32[2,128]{1,0:T(2,128)S(1)} %get-tuple-element.22, f32[24,15,15]{2,1,0:T(8,128)S(1)} %reshape.285), channel_id=1, replica_groups=mesh['row'=16,'col'=2] {'col'}, use_global_device_ids=true, to_apply=%region_14.15 | all-reduce | flops 5656 | bytes 45248 | tf_op jit(solution)/shard_map/psum | solution.py:170
  262.6 0.8 copy.72
  263.4 4.0 %fusion.6 = bf16[16,8,4,3072]{3,1,0,2:T(8,128)(2,1)S(1)} fusion(s32[]{:T(128)S(6)} %select_n.80, bf16[16,8,4,3072]{3,1,0,2:T(8,128)(2,1)} %collective-permute-done.3, bf16[16,8,4,3072]{3,1,0,2:T(8,128)(2,1)S(1)} %fusion.3), kind=kLoop, calls=%fused_computation.16 | loop fusion | flops 6291456 | bytes 9437188 | tf_op jit(solution)/shard_map/concatenate | solution.py:165
  267.5 0.9 slice_bitcast_fusion
  268.4 0.2 slice.58
  268.6 1.6 copy.71
  (57 shorter events, 0.7 us)
Async XLA Ops:
  0.6 7.1 %copy-start.16 = (s32[2]{0:T(128)S(1)}, s32[2]{0:T(128)}, u32[]{:S(2)}) copy-start(s32[2]{0:T(128)} %param.10) | copy-start | bytes 28
  2.2 23.4 %collective-permute-start = (bf16[8,8,4,3072]{3,1,2,0:T(8,128)(2,1)S(1)}, bf16[8,8,4,3072]{3,1,2,0:T(8,128)(2,1)}, u32[]{:S(2)}, u32[]{:S(2)}) collective-permute-start(bf16[8,8,4,3072]{3,1,2,0:T(8,128)(2,1)S(1)} %pad_maximum_fusion), channel_id=1, source_target_pairs={{0,30},{2,0},{4,2},{6,4},{8,6},{10,8},{12,10},{14,12},{16,14},{18,... | collective-permute-start | bytes 4718600 | tf_op jit(solution)/shard_map/ppermute | solution.py:14
  10.2 22.3 %copy-start.14 = (s32[256,16]{0,1:T(8,128)S(1)}, s32[256,16]{0,1:T(8,128)}, u32[]{:S(2)}) copy-start(s32[256,16]{0,1:T(8,128)} %param.11) | copy-start | bytes 49156
  10.2 22.5 %copy-start.13 = (f32[24,15,15]{0,2,1:T(8,128)S(1)}, f32[24,15,15]{0,2,1:T(8,128)}, u32[]{:S(2)}) copy-start(f32[24,15,15]{0,2,1:T(8,128)} %param.9) | copy-start | bytes 64804
  28.5 68.1 %collective-permute-start.1 = (bf16[16,8,4,3072]{3,1,2,0:T(8,128)(2,1)S(1)}, bf16[16,8,4,3072]{3,1,2,0:T(8,128)(2,1)}, u32[]{:S(2)}, u32[]{:S(2)}) collective-permute-start(bf16[16,8,4,3072]{3,1,2,0:T(8,128)(2,1)S(1)} %fusion.5), channel_id=1, source_target_pairs={{0,1},{1,0},{2,3},{3,2},{4,5},{5,4},{6,7},{7,6},{8,9},{9,8},{10,11... | collective-permute-start | bytes 9437192 | tf_op jit(solution)/shard_map/ppermute | solution.py:14
  32.9 0.6 copy-start.11
  38.9 2.9 %copy-start.15 = (f32[2,128]{1,0:T(2,128)S(1)}, f32[2,128]{1,0:T(2,128)}, u32[]{:S(2)}) copy-start(f32[2,128]{1,0:T(2,128)} %param.8) | copy-start | bytes 3076
  111.2 1.7 copy-start.2
  129.5 2.6 copy-start.1
  132.1 1.4 copy-start.3
  132.1 2.2 copy-start.4
  132.1 2.1 copy-start.20
  134.2 4.8 %copy-start.19 = (f32[128]{0:T(128)S(1)}, f32[128]{0:T(128)}, u32[]{:S(2)}) copy-start(f32[128]{0:T(128)} %get-tuple-element.35) | copy-start | bytes 1540
  151.5 1.4 copy-start.8
  153.2 0.9 copy-start.9
  153.2 0.9 copy-start.10
  159.2 1.6 copy-start.7
  159.2 1.9 copy-start.6
  161.2 1.1 copy-start.5
  162.4 1.7 copy-start
  164.1 22.6 %collective-permute-start.2 = (bf16[8,8,4,3072]{3,1,0,2:T(8,128)(2,1)S(1)}, bf16[8,8,4,3072]{3,1,0,2:T(8,128)(2,1)}, u32[]{:S(2)}, u32[]{:S(2)}) collective-permute-start(bf16[8,8,4,3072]{3,1,0,2:T(8,128)(2,1)S(1)} %slice.56), channel_id=1, source_target_pairs={{0,2},{2,4},{4,6},{6,8},{8,10},{10,12},{12,14},{14,16},{16,18},{18... | collective-permute-start | bytes 4718600 | tf_op jit(solution)/shard_map/ppermute | solution.py:14
  165.4 26.7 %copy-start.17 = (f32[128]{0:T(128)S(1)}, f32[128]{0:T(128)}, u32[]{:S(2)}) copy-start(f32[128]{0:T(128)} %get-tuple-element.14) | copy-start | bytes 1540
  165.4 26.7 %copy-start.18 = (f32[128]{0:T(128)S(1)}, f32[128]{0:T(128)}, u32[]{:S(2)}) copy-start(f32[128]{0:T(128)} %get-tuple-element.12) | copy-start | bytes 1540
  165.4 26.7 %copy-start.12 = (s32[64,64]{0,1:T(8,128)S(1)}, s32[64,64]{0,1:T(8,128)}, u32[]{:S(2)}) copy-start(s32[64,64]{0,1:T(8,128)} %copy-done.11) | copy-start | bytes 49156
  189.3 74.1 %collective-permute-start.3 = (bf16[16,8,4,3072]{3,1,0,2:T(8,128)(2,1)S(1)}, bf16[16,8,4,3072]{3,1,0,2:T(8,128)(2,1)}, u32[]{:S(2)}, u32[]{:S(2)}) collective-permute-start(bf16[16,8,4,3072]{3,1,0,2:T(8,128)(2,1)S(1)} %fusion.3), channel_id=1, source_target_pairs={{0,1},{1,0},{2,3},{3,2},{4,5},{5,4},{6,7},{7,6},{8,9},{9,8},{10,11... | collective-permute-start | bytes 9437192 | tf_op jit(solution)/shard_map/ppermute | solution.py:14
